TPU v7x, 32 devices: a whole 2x2x4 slice. The times are simulated.
32 devices in a mesh: row: 4 (over x, core), col: 4 (over z), vir: 2 (over y).
Axes of the slice: x: 2, y: 2, z: 4, core: 2. Of those that a mesh axis runs over, the one named last changes fastest.
Arguments:
- amplitudes: float32 [80, 4, 4, 3, 128, 128], P('vir', 'row', 'col'), may hold values from -6 to 6
- integrals: float32 [80, 4, 4, 3, 128, 128], P('vir', 'row', 'col'), may hold values from -6 to 6
- cycle_terms: float32 [80, 4, 4, 3, 128, 128], P('vir', 'row', 'col'), may hold values from -0.15625 to 0.15625
- ladder_factors: float32 [80, 8, 128, 128], P('vir'), may hold values from -0.375 to 0.375
- live: int32 [80, 4, 4, 3], P('vir', 'row', 'col'), may hold values 0 or 1
Outputs:
- residual: float32 [80, 4, 4, 3, 128, 128], P('vir', 'row', 'col')
All inputs are finite; a program needn't handle non-finite values. No bound on the sum of `live` on one device may be relied on, other than what follows from the above.
Results may differ from a plain program's by a relative error of at most 0.0001.
Values sent between devices are 32-bit elements; how exact they have to be, the bound alone decides.
No kernel may reach another device: no remote copies, remote signals or barrier semaphores. Data moves between devices by JAX's collectives and lax.ppermute only.
A program may use at most 448 MiB of HBM per device.

v0:
```python
import jax
import jax.numpy as jnp
from jax import lax
from jax.sharding import PartitionSpec as P

NT = 80


def extended(block, sides, width):
    for axis, dim in sides:
        count = lax.axis_size(axis)
        forward = [(i, i + 1) for i in range(count - 1)]
        backward = [(target, source) for source, target in forward]
        low = lax.ppermute(
            lax.slice_in_dim(block, block.shape[dim] - width, None, axis=dim), axis, forward
        )
        high = lax.ppermute(lax.slice_in_dim(block, 0, width, axis=dim), axis, backward)
        block = jnp.concatenate([low, block, high], axis=dim)
    return block


def per_device(amplitudes, integrals, cycle_terms, ladder_factors, live):
    local_tiles = amplitudes.shape[0]
    occupied = amplitudes.shape[1]
    band_slots = amplitudes.shape[3]
    tile_size = amplitudes.shape[4]
    factor_count = ladder_factors.shape[1]
    half_band = band_slots // 2
    slot_index = jnp.arange(band_slots)
    global_rows = lax.axis_index("vir") * local_tiles + jnp.arange(local_tiles)
    col_tile = global_rows[:, None] + slot_index[None, :] - half_band
    inside = (col_tile >= 0) & (col_tile < NT)
    keep = ((live == 1) | (slot_index == half_band)[None, None, None, :]) & inside[:, None, None, :]
    keep_float = keep.astype(jnp.float32)[..., None, None]
    amps = amplitudes * keep_float
    pair_tiles = occupied * occupied * band_slots
    joined = jnp.concatenate(
        [cycle_terms.reshape(local_tiles, pair_tiles, tile_size, tile_size), ladder_factors], axis=1
    )
    widened = extended(joined, (("vir", 0),), half_band)
    cycle_ext = widened[:, :pair_tiles].reshape(
        local_tiles + 2 * half_band, occupied, occupied, band_slots, tile_size, tile_size
    )
    factors = widened[:, pair_tiles:]
    cycle_all = lax.all_gather(cycle_ext, "row", axis=1, tiled=True)
    centre = factors[half_band : half_band + local_tiles]
    ladder = jnp.zeros(amplitudes.shape, jnp.float32)
    for term_index in range(factor_count):
        inner = jnp.einsum(
            "axy,aijsyz->aijsxz", centre[:, term_index], amps, precision=lax.Precision.HIGHEST
        )
        parts = []
        for out_slot in range(band_slots):
            right_side = factors[out_slot : out_slot + local_tiles, term_index]
            parts.append(
                jnp.einsum(
                    "aijxz,awz->aijxw",
                    inner[:, :, :, out_slot],
                    right_side,
                    precision=lax.Precision.HIGHEST,
                )
            )
        ladder = ladder + jnp.stack(parts, axis=3)
    piece = lax.all_gather(amps, "col", axis=2, tiled=True)
    slot_sums = []
    for out_slot in range(band_slots):
        summed = jnp.zeros((local_tiles, occupied, occupied, tile_size, tile_size), jnp.float32)
        for in_slot in range(band_slots):
            mid_slot = out_slot - in_slot + half_band
            if 0 <= mid_slot < band_slots:
                cycle_rows = cycle_all[in_slot : in_slot + local_tiles, :, :, mid_slot]
                summed = summed + jnp.einsum(
                    "aiktu,akjuv->aijtv",
                    piece[:, :, :, in_slot],
                    cycle_rows,
                    precision=lax.Precision.HIGHEST,
                )
        slot_sums.append(summed)
    cycle = jnp.stack(slot_sums, axis=3)
    return keep_float * (integrals + ladder + cycle)


def solution(mesh):
    in_specs = (
        P("vir", "row", "col", None, None, None),
        P("vir", "row", "col", None, None, None),
        P("vir", "row", "col", None, None, None),
        P("vir", None, None, None),
        P("vir", "row", "col", None),
    )
    out_specs = P("vir", "row", "col", None, None, None)
    return jax.shard_map(
        per_device, mesh=mesh, in_specs=in_specs, out_specs=out_specs, check_vma=False
    )
```

profile of v0, /device:TPU:0, one launch (start us, length us, event | category | flops | bytes accessed | tf_op | source)
XLA Modules:
  0.0 918.6 jit_solution(8032832479250462117)
XLA Ops:
  21.2 4.9 collective-permute-start
  27.4 14.0 %collective-permute-done = f32[1,11,128,128]{3,2,0,1:T(8,128)S(1)} collective-permute-done((f32[1,11,128,128]{3,2,0,1:T(8,128)S(1)}, f32[1,11,128,128]{3,2,0,1:T(8,128)S(1)}, u32[]{:S(2)}, u32[]{:S(2)}) %collective-permute-start) | collective-permute-done | bytes 720928 | tf_op jit(solution)/shard_map/ppermute | solution.py:14
  41.5 4.2 collective-permute-done.1
  45.6 4.2 pad_maximum_fusion
  49.9 17.9 %fusion.32 = f32[40,1,1,3,128,128]{4,5,3,0,2,1:T(8,128)S(1)} fusion(f32[40,3]{0,1:T(4,128)S(1)} %bitcast.514, f32[40,1,1,3,128,128]{5,4,3,2,1,0:T(8,128)} %param.5, f32[40,8,128,128]{3,2,1,0:T(8,128)} %param.8), kind=kOutput, calls=%fused_computation.48 | convolution fusion | flops 3021864960 | bytes 18350560 | tf_op jit(solution)/shard_map/axy,aijsyz->aijsxz/dot_general | solution.py:49
  71.0 8.0 fusion.178
  79.1 18.1 %fusion.35 = f32[40,1,1,3,128,128]{4,5,3,0,2,1:T(8,128)} fusion(f32[40,3]{0,1:T(4,128)S(1)} %bitcast.515, f32[40,1,1,3,128,128]{5,4,3,2,1,0:T(8,128)} %param.5, f32[40,8,128,128]{3,2,1,0:T(8,128)} %param.8), kind=kOutput, calls=%fused_computation.49 | convolution fusion | flops 3021864960 | bytes 18350560 | tf_op jit(solution)/shard_map/axy,aijsyz->aijsxz/dot_general | solution.py:49
  97.2 7.6 fusion.183
  104.9 15.8 %fusion.38 = f32[40,1,1,3,128,128]{4,5,3,0,2,1:T(8,128)} fusion(f32[40,3]{0,1:T(4,128)S(1)} %bitcast.516, f32[40,1,1,3,128,128]{5,4,3,2,1,0:T(8,128)S(1)} %bitcast.501, f32[40,8,128,128]{3,2,1,0:T(8,128)S(1)} %bitcast.499), kind=kOutput, calls=%fused_computation.50 | convolution fusion | flops 3021864960 | bytes 18352128 | tf_op jit(solution)/shard_map/axy,aijsyz->aijsxz/dot_general | solution.py:49
  120.7 7.7 fusion.188
  128.3 15.5 %fusion.41 = f32[40,1,1,3,128,128]{4,5,3,0,2,1:T(8,128)} fusion(f32[40,3]{0,1:T(4,128)S(1)} %bitcast.517, f32[40,1,1,3,128,128]{5,4,3,2,1,0:T(8,128)S(1)} %bitcast.501, f32[40,8,128,128]{3,2,1,0:T(8,128)S(1)} %bitcast.499), kind=kOutput, calls=%fused_computation.51 | convolution fusion | flops 3021864960 | bytes 18352128 | tf_op jit(solution)/shard_map/axy,aijsyz->aijsxz/dot_general | solution.py:49
  143.9 7.7 fusion.193
  151.6 15.6 %fusion.44 = f32[40,1,1,3,128,128]{4,5,3,0,2,1:T(8,128)} fusion(f32[40,3]{0,1:T(4,128)S(1)} %bitcast.518, f32[40,1,1,3,128,128]{5,4,3,2,1,0:T(8,128)S(1)} %bitcast.501, f32[40,8,128,128]{3,2,1,0:T(8,128)S(1)} %bitcast.499), kind=kOutput, calls=%fused_computation.52 | convolution fusion | flops 3021864960 | bytes 18352128 | tf_op jit(solution)/shard_map/axy,aijsyz->aijsxz/dot_general | solution.py:49
  167.2 7.7 fusion.198
  174.9 15.9 %fusion.47 = f32[40,1,1,3,128,128]{4,5,3,0,2,1:T(8,128)} fusion(f32[40,3]{0,1:T(4,128)S(1)} %bitcast.519, f32[40,1,1,3,128,128]{5,4,3,2,1,0:T(8,128)S(1)} %bitcast.501, f32[40,8,128,128]{3,2,1,0:T(8,128)S(1)} %bitcast.499), kind=kOutput, calls=%fused_computation.53 | convolution fusion | flops 3021864960 | bytes 18352128 | tf_op jit(solution)/shard_map/axy,aijsyz->aijsxz/dot_general | solution.py:49
  190.7 7.7 fusion.203
  198.5 15.6 %fusion.50 = f32[40,1,1,3,128,128]{4,5,3,0,2,1:T(8,128)} fusion(f32[40,3]{0,1:T(4,128)S(1)} %bitcast.520, f32[40,1,1,3,128,128]{5,4,3,2,1,0:T(8,128)S(1)} %bitcast.501, f32[40,8,128,128]{3,2,1,0:T(8,128)S(1)} %bitcast.499), kind=kOutput, calls=%fused_computation.54 | convolution fusion | flops 3021864960 | bytes 18352128 | tf_op jit(solution)/shard_map/axy,aijsyz->aijsxz/dot_general | solution.py:49
  214.0 7.9 fusion.208
  221.9 18.1 %fusion.53 = f32[40,1,1,3,128,128]{4,5,3,0,2,1:T(8,128)} fusion(f32[40,3]{0,1:T(4,128)S(1)} %bitcast.521, f32[40,1,1,3,128,128]{5,4,3,2,1,0:T(8,128)} %param.5, f32[40,8,128,128]{3,2,1,0:T(8,128)S(1)} %bitcast.499), kind=kOutput, calls=%fused_computation.55 | convolution fusion | flops 3021864960 | bytes 18352128 | tf_op jit(solution)/shard_map/axy,aijsyz->aijsxz/dot_general | solution.py:49
  240.0 7.6 fusion.215
  247.6 7.7 fusion.182
  255.3 7.8 fusion.186
  263.2 7.7 fusion.187
  270.9 7.7 fusion.191
  278.6 7.9 fusion.192
  286.5 7.7 fusion.196
  294.2 7.7 fusion.197
  301.8 8.1 fusion.201
  309.9 7.6 fusion.202
  317.6 7.8 fusion.206
  325.4 7.7 fusion.207
  333.0 7.7 fusion.211
  340.7 7.9 fusion.212
  348.6 7.7 fusion.218
  356.3 7.7 fusion.177
  363.9 8.1 fusion.181
  372.0 173.2 %all-gather.4.cloned.1.call-done = f32[40,1,4,3,128,128]{5,4,3,1,0,2:T(8,128)} async-done(((f32[40,1,1,3,128,128]{5,4,3,1,0,2:T(8,128)}), f32[40,1,4,3,128,128]{5,4,3,1,0,2:T(8,128)}) %all-gather.4.cloned.1.call-update) | async-done | bytes 31457296 | tf_op jit(solution)/shard_map/all_gather | solution.py:64
  545.2 25.9 %fusion.237 = (f32[40,1,4,1,128,128]{5,4,3,1,0,2:T(8,128)}, f32[40,1,4,1,128,128]{5,4,3,1,0,2:T(8,128)}, f32[40,1,4,1,128,128]{5,4,3,1,0,2:T(8,128)}) fusion(f32[40,1,4,3,128,128]{5,4,3,1,0,2:T(8,128)} %all-gather.4.cloned.1.call-done), kind=kLoop, calls=%fused_computation.267 | loop fusion | bytes 62914560 | tf_op jit(solution)/shard_map/slice | solution.py:74
  571.1 172.4 %all-gather.6.cloned.1.call-done = f32[42,12,128,128]{3,2,0,1:T(8,128)} async-done(((f32[42,3,128,128]{3,2,0,1:T(8,128)}), f32[42,12,128,128]{3,2,0,1:T(8,128)}) %all-gather.6.cloned.1.call-update) | async-done | bytes 33030160 | tf_op jit(solution)/shard_map/all_gather | solution.py:45
  743.6 24.3 %copy.172 = f32[42,12,128,128]{3,2,1,0:T(8,128)} copy(f32[42,12,128,128]{3,2,0,1:T(8,128)} %all-gather.6.cloned.1.call-done) | data formatting | bytes 66060288 | tf_op jit(solution)/shard_map/all_gather | solution.py:45
  768.2 15.4 %fusion.4 = f32[40,128,128,1]{1,2,3,0:T(8,128)} fusion(f32[42,4,1,3,128,128]{5,4,3,1,0,2:T(8,128)} %bitcast.502, f32[40,1,4,1,128,128]{5,4,3,1,0,2:T(8,128)S(1)} %copy-done.1), kind=kOutput, calls=%fused_computation.9 | convolution fusion | flops 4026531840 | bytes 23592960 | tf_op jit(solution)/shard_map/aiktu,akjuv->aijtv/dot_general | solution.py:72
  783.6 16.2 %fusion.6 = f32[40,128,128,1]{1,2,3,0:T(8,128)S(1)} fusion(f32[42,4,1,3,128,128]{5,4,3,1,0,2:T(8,128)} %bitcast.503, f32[40,1,4,1,128,128]{5,4,3,1,0,2:T(8,128)} %get-tuple-element.5), kind=kOutput, calls=%fused_computation.13 | convolution fusion | flops 4026531840 | bytes 23592960 | tf_op jit(solution)/shard_map/aiktu,akjuv->aijtv/dot_general | solution.py:72
  799.9 15.3 %fusion.3 = f32[40,128,128,1]{1,2,3,0:T(8,128)} fusion(f32[42,4,1,3,128,128]{5,4,3,1,0,2:T(8,128)} %bitcast.504, f32[40,1,4,1,128,128]{5,4,3,1,0,2:T(8,128)S(1)} %bitcast.510), kind=kOutput, calls=%fused_computation.7 | convolution fusion | flops 4026531840 | bytes 23592960 | tf_op jit(solution)/shard_map/aiktu,akjuv->aijtv/dot_general | solution.py:72
  815.2 15.4 %fusion.1 = f32[40,128,128,1]{1,2,3,0:T(8,128)} fusion(f32[42,4,1,3,128,128]{5,4,3,1,0,2:T(8,128)} %bitcast.505, f32[40,1,4,1,128,128]{5,4,3,1,0,2:T(8,128)S(1)} %bitcast.510), kind=kOutput, calls=%fused_computation.3 | convolution fusion | flops 4026531840 | bytes 23592960 | tf_op jit(solution)/shard_map/aiktu,akjuv->aijtv/dot_general | solution.py:72
  830.6 15.6 %fusion.152 = f32[40,1,1,1,128,128]{5,4,0,3,2,1:T(8,128)} fusion(f32[40,128,128,1]{1,2,3,0:T(8,128)S(1)} %fusion.6, f32[40,1,4,1,128,128]{5,4,3,1,0,2:T(8,128)S(1)} %bitcast.510, f32[42,4,1,3,128,128]{5,4,3,1,0,2:T(8,128)} %bitcast.506), kind=kOutput, calls=%fused_computation.196 | convolution fusion | flops 4027187200 | bytes 26214400 | tf_op jit(solution)/shard_map/aiktu,akjuv->aijtv/dot_general | solution.py:72
  846.2 20.5 %fusion.150 = f32[40,1,1,1,128,128]{5,4,0,3,2,1:T(8,128)} fusion(f32[40,128,128,1]{1,2,3,0:T(8,128)} %fusion.1, f32[40,1,4,1,128,128]{5,4,3,1,0,2:T(8,128)} %get-tuple-element.7, f32[42,4,1,3,128,128]{5,4,3,1,0,2:T(8,128)} %bitcast.507), kind=kOutput, calls=%fused_computation.191 | convolution fusion | flops 4027187200 | bytes 26214400 | tf_op jit(solution)/shard_map/aiktu,akjuv->aijtv/dot_general | solution.py:72
  866.7 16.1 %fusion.151 = f32[40,1,1,1,128,128]{5,4,0,3,2,1:T(8,128)} fusion(f32[40,128,128,1]{1,2,3,0:T(8,128)} %fusion.3, f32[40,128,128,1]{1,2,3,0:T(8,128)S(1)} %copy-done.4, f32[40,1,4,1,128,128]{5,4,3,1,0,2:T(8,128)S(1)} %bitcast.512, f32[42,4,1,3,128,128]{5,4,3,1,0,2:T(8,128)} %bitcast.508), kind=kOutput, calls=%fused_computation.193 | convolution fusion | flops 4027842560 | bytes 28835840 | tf_op jit(solution)/shard_map/aiktu,akjuv->aijtv/dot_general | solution.py:72
  882.9 25.0 %fusion.15 = f32[40,1,1,3,128,128]{5,4,0,3,2,1:T(8,128)S(1)} fusion(f32[40,1,1,1,128,128]{5,4,0,3,2,1:T(8,128)} %fusion.181, f32[40,1,1,1,128,128]{5,4,0,3,2,1:T(8,128)} %fusion.178, f32[40,1,1,1,128,128]{5,4,0,3,2,1:T(8,128)} %fusion.177, f32[40,1,1,1,128,128]{5,4,0,3,2,1:T(8,128)} %fusion.186, f32[40,1,1,1,128,128]{5,4,0,3,2,1:T(8,128)} %fusion.183, ...), kind=kLoop, calls=%fused_computation.29 | loop fusion | flops 55050240 | bytes 86508000 | tf_op jit(solution)/shard_map/mul | solution.py:80
  (63 shorter events, 23.3 us)
Async XLA Ops:
  6.5 538.7 %all-gather.4.cloned.1.call-start = ((), (), s32[]{:S(2)}) async-start(), calls=%async_computation | async-start | bytes 39321600 | tf_op jit(solution)/shard_map/all_gather | solution.py:64
  7.3 214.6 %copy-start.5 = (f32[40,1,1,3]{0,3,2,1:T(4,128)}, f32[40,1,1,3]{0,3,2,1:T(4,128)S(1)}, u32[]{:S(2)}) copy-start(f32[40,1,1,3]{0,3,2,1:T(4,128)S(1)} %copy.436) | copy-start | bytes 1444
  15.3 728.3 %all-gather.6.cloned.1.call-start = ((), (), s32[]{:S(2)}) async-start(), calls=%async_computation.1 | async-start | bytes 41287680 | tf_op jit(solution)/shard_map/all_gather | solution.py:45
  19.1 26.5 %copy-start = (f32[40,1,1,3,128,128]{5,4,0,3,2,1:T(8,128)}, f32[40,1,1,3,128,128]{5,4,0,3,2,1:T(8,128)S(1)}, u32[]{:S(2)}) copy-start(f32[40,1,1,3,128,128]{5,4,0,3,2,1:T(8,128)S(1)} %copy.435) | copy-start | bytes 23592964
  21.2 20.3 %collective-permute-start = (f32[1,11,128,128]{3,2,0,1:T(8,128)S(1)}, f32[1,11,128,128]{3,2,0,1:T(8,128)S(1)}, u32[]{:S(2)}, u32[]{:S(2)}) collective-permute-start(f32[1,11,128,128]{3,2,0,1:T(8,128)S(1)} %get-tuple-element.8), channel_id=1, source_target_pairs={{0,1},{2,3},{4,5},{6,7},{8,9},{10,11},{12,13},{14,15},{16,17},{18,... | collective-permute-start | bytes 2162696 | tf_op jit(solution)/shard_map/ppermute | solution.py:14
  26.1 19.5 %collective-permute-start.1 = (f32[1,11,128,128]{3,2,0,1:T(8,128)S(1)}, f32[1,11,128,128]{3,2,0,1:T(8,128)S(1)}, u32[]{:S(2)}, u32[]{:S(2)}) collective-permute-start(f32[1,11,128,128]{3,2,0,1:T(8,128)S(1)} %get-tuple-element.9), channel_id=1, source_target_pairs={{1,0},{3,2},{5,4},{7,6},{9,8},{11,10},{13,12},{15,14},{17,16},{19,... | collective-permute-start | bytes 2162696 | tf_op jit(solution)/shard_map/ppermute | solution.py:17
  49.9 47.3 %slice-start.2 = ((s8[20971520]{0:T(1024)(128)(4,1)}), s8[4194304]{0:T(1024)(128)(4,1)S(1)}, s32[]{:S(2)}) async-start(s8[20971520]{0:T(1024)(128)(4,1)} %bitcast.498), calls=%async_computation.4 | async-start | bytes 8388608
  49.9 47.3 %slice-start.3 = ((s8[20971520]{0:T(1024)(128)(4,1)}), s8[4194304]{0:T(1024)(128)(4,1)S(1)}, s32[]{:S(2)}) async-start(s8[20971520]{0:T(1024)(128)(4,1)} %bitcast.498), calls=%async_computation.5 | async-start | bytes 8388608
  49.9 47.3 %slice-start.4 = ((s8[20971520]{0:T(1024)(128)(4,1)}), s8[4194304]{0:T(1024)(128)(4,1)S(1)}, s32[]{:S(2)}) async-start(s8[20971520]{0:T(1024)(128)(4,1)} %bitcast.498), calls=%async_computation.6 | async-start | bytes 8388608
  67.8 3.2 copy-start.2
  71.0 33.9 %slice-start.7 = ((s8[7864320]{0:T(1024)(128)(4,1)}), s8[4194304]{0:T(1024)(128)(4,1)S(1)}, s32[]{:S(2)}) async-start(s8[7864320]{0:T(1024)(128)(4,1)} %bitcast.500), calls=%async_computation.9 | async-start | bytes 8388608
  79.1 18.1 %slice-start.5 = ((s8[20971520]{0:T(1024)(128)(4,1)}), s8[4194304]{0:T(1024)(128)(4,1)S(1)}, s32[]{:S(2)}) async-start(s8[20971520]{0:T(1024)(128)(4,1)} %bitcast.498), calls=%async_computation.7 | async-start | bytes 8388608
  79.1 18.2 %slice-start.6 = ((s8[20971520]{0:T(1024)(128)(4,1)}), s8[4194304]{0:T(1024)(128)(4,1)S(1)}, s32[]{:S(2)}) async-start(s8[20971520]{0:T(1024)(128)(4,1)} %bitcast.498), calls=%async_computation.8 | async-start | bytes 8388608
  79.1 25.8 %slice-start.8 = ((s8[7864320]{0:T(1024)(128)(4,1)}), s8[3670016]{0:T(1024)(128)(4,1)S(1)}, s32[]{:S(2)}) async-start(s8[7864320]{0:T(1024)(128)(4,1)} %bitcast.500), calls=%async_computation.10 | async-start | bytes 7340032
  214.0 33.6 %slice-start = ((s8[7864320]{0:T(1024)(128)(4,1)}), s8[4194304]{0:T(1024)(128)(4,1)S(1)}, s32[]{:S(2)}) async-start(s8[7864320]{0:T(1024)(128)(4,1)} %bitcast.480), calls=%async_computation.2 | async-start | bytes 8388608
  221.9 25.7 %slice-start.1 = ((s8[7864320]{0:T(1024)(128)(4,1)}), s8[3670016]{0:T(1024)(128)(4,1)S(1)}, s32[]{:S(2)}) async-start(s8[7864320]{0:T(1024)(128)(4,1)} %bitcast.480), calls=%async_computation.3 | async-start | bytes 7340032
  743.6 24.7 %copy-start.1 = (f32[40,1,4,1,128,128]{5,4,3,1,0,2:T(8,128)S(1)}, f32[40,1,4,1,128,128]{5,4,3,1,0,2:T(8,128)}, u32[]{:S(2)}) copy-start(f32[40,1,4,1,128,128]{5,4,3,1,0,2:T(8,128)} %get-tuple-element.5) | copy-start | bytes 31457284
  768.2 31.7 %slice-start.9 = ((s8[10485760]{0:T(1024)(128)(4,1)}), s8[4194304]{0:T(1024)(128)(4,1)S(1)}, s32[]{:S(2)}) async-start(s8[10485760]{0:T(1024)(128)(4,1)} %bitcast.509), calls=%async_computation.11 | async-start | bytes 8388608
  768.2 31.7 %slice-start.10 = ((s8[10485760]{0:T(1024)(128)(4,1)}), s8[4194304]{0:T(1024)(128)(4,1)S(1)}, s32[]{:S(2)}) async-start(s8[10485760]{0:T(1024)(128)(4,1)} %bitcast.509), calls=%async_computation.12 | async-start | bytes 8388608
  783.6 16.3 %slice-start.11 = ((s8[10485760]{0:T(1024)(128)(4,1)}), s8[2097152]{0:T(1024)(128)(4,1)S(1)}, s32[]{:S(2)}) async-start(s8[10485760]{0:T(1024)(128)(4,1)} %bitcast.509), calls=%async_computation.13 | async-start | bytes 4194304
  830.6 36.1 %slice-start.12 = ((s8[10485760]{0:T(1024)(128)(4,1)}), s8[2097152]{0:T(1024)(128)(4,1)S(1)}, s32[]{:S(2)}) async-start(s8[10485760]{0:T(1024)(128)(4,1)} %bitcast.511), calls=%async_computation.14 | async-start | bytes 4194304
  830.6 36.1 %slice-start.13 = ((s8[10485760]{0:T(1024)(128)(4,1)}), s8[4194304]{0:T(1024)(128)(4,1)S(1)}, s32[]{:S(2)}) async-start(s8[10485760]{0:T(1024)(128)(4,1)} %bitcast.511), calls=%async_computation.15 | async-start | bytes 8388608
  846.2 20.5 %slice-start.14 = ((s8[10485760]{0:T(1024)(128)(4,1)}), s8[4194304]{0:T(1024)(128)(4,1)S(1)}, s32[]{:S(2)}) async-start(s8[10485760]{0:T(1024)(128)(4,1)} %bitcast.511), calls=%async_computation.16 | async-start | bytes 8388608
  846.2 20.5 %copy-start.4 = (f32[40,128,128,1]{1,2,3,0:T(8,128)S(1)}, f32[40,128,128,1]{1,2,3,0:T(8,128)}, u32[]{:S(2)}) copy-start(f32[40,128,128,1]{1,2,3,0:T(8,128)} %fusion.4) | copy-start | bytes 7864324
  866.7 16.2 %copy-start.3 = (f32[40,1,1,1,128,128]{5,4,0,3,2,1:T(8,128)S(1)}, f32[40,1,1,1,128,128]{5,4,0,3,2,1:T(8,128)}, u32[]{:S(2)}) copy-start(f32[40,1,1,1,128,128]{5,4,0,3,2,1:T(8,128)} %fusion.182) | copy-start | bytes 7864324
  866.7 16.1 %copy-start.6 = (f32[40,1,1,3]{0,3,2,1:T(4,128)S(1)}, f32[40,1,1,3]{0,3,2,1:T(4,128)}, u32[]{:S(2)}) copy-start(f32[40,1,1,3]{0,3,2,1:T(4,128)} %copy-done.5) | copy-start | bytes 1444
Sparse Core Ops, SparseCore 0:
  15.4 529.8 all-gather.3
  546.8 196.6 all-gather.5
where the time goes:
time: 922 us; the launch traced here: 919 us
  matrix products  433 us (47%)
  waiting for transfers between devices  364 us (39%)
  local copies, waits for them, and re-layouts  65.5 us (7%)
  other arithmetic  35.8 us (4%)
  between operations  13.8 us (1%)
    dot_general x24, matrix products, per_device(): jnp.einsum('aijxz,awz->aijxw', inner[:, :, :, out_slot], right_side, prec...  186 us
    all_gather x1, waiting for transfers between devices, per_device(): piece = lax.all_gather(amps, 'col', axis=2, tiled=True)  173 us
    all_gather x1, waiting for transfers between devices, per_device(): cycle_all = lax.all_gather(cycle_ext, 'row', axis=1, tiled=True)  172 us
    dot_general x8, matrix products, per_device(): jnp.einsum('axy,aijsyz->aijsxz', centre[:, term_index], amps, precision=l...  132 us
    dot_general x7, matrix products, per_device(): jnp.einsum('aiktu,akjuv->aijtv', piece[:, :, :, in_slot], cycle_rows, pre...  115 us
    slice x1, local copies, waits for them, and re-layouts, per_device(): piece[:, :, :, in_slot]  25.9 us
    mul x2, other arithmetic, per_device(): return keep_float * (integrals + ladder + cycle)  25.7 us
    all_gather x1, local copies, waits for them, and re-layouts, per_device(): cycle_all = lax.all_gather(cycle_ext, 'row', axis=1, tiled=True)  24.3 us
  transfers between devices with their start and end apart: 4, of which 4 were waited for; matrix products, arithmetic and copies ran while one was open for 39% of the time, Pallas kernels for 0%

commit v1 on v0

--- a/solution.py
+++ b/solution.py
@@ -1,9 +1,29 @@
+import functools
 import jax
 import jax.numpy as jnp
 from jax import lax
 from jax.sharding import PartitionSpec as P
 
 NT = 80
+
+
+def field_plan(incoming_x, mesh_name):
+    count_all = lax.axis_size(mesh_name)
+    x_new = sorted(((j, (j + 1) % count_all) for j in range(count_all)))
+    piece_now = incoming_x
+    copies = [piece_now]
+    dd = 1
+    while dd < count_all:
+        piece_now = lax.ppermute(piece_now, axis_name=mesh_name, perm=x_new)
+        copies.insert(0, piece_now)
+        dd += 1
+    shaped = jnp.concatenate(copies, 1)
+    upper = lax.axis_index(mesh_name)
+    piece_next = upper + 1
+    return jnp.roll(shaped, piece_next * incoming_x.shape[1], 1)
+
+
+local_data_touch = functools.partial(field_plan, mesh_name="row")
 
 
 def extended(block, sides, width):
@@ -42,7 +62,7 @@
         local_tiles + 2 * half_band, occupied, occupied, band_slots, tile_size, tile_size
     )
     factors = widened[:, pair_tiles:]
-    cycle_all = lax.all_gather(cycle_ext, "row", axis=1, tiled=True)
+    cycle_all = local_data_touch(cycle_ext)
     centre = factors[half_band : half_band + local_tiles]
     ladder = jnp.zeros(amplitudes.shape, jnp.float32)
     for term_index in range(factor_count):

time: 922 us -> 705 us (0.76)
  waiting for transfers between devices: 364 us -> 135 us
    all_gather x1 -> x0, waiting for transfers between devices: 172 us -> none  [per_device(): cycle_all = lax.all_gather(cycle_ext, 'row', axis=1, tiled=True)]
    all_gather x1, waiting for transfers between devices: 173 us -> 25.1 us  [per_device(): piece = lax.all_gather(amps, 'col', axis=2, tiled=True)]
    ppermute x0 -> x3, waiting for transfers between devices: none -> 91.6 us  [field_plan(): piece_now = lax.ppermute(piece_now, axis_name=mesh_name, perm=x_new)]
    unnamed x46 -> x53, local copies, waits for them, and re-layouts: 7.45 us -> 60.3 us
    slice x1 -> x0, local copies, waits for them, and re-layouts: 25.9 us -> none  [per_device(): piece[:, :, :, in_slot]]
    all_gather x1 -> x0, local copies, waits for them, and re-layouts: 24.3 us -> none  [per_device(): cycle_all = lax.all_gather(cycle_ext, 'row', axis=1, tiled=True)]
  transfers between devices with their start and end apart: 4 -> 6, of which waited for: 4 -> 4; matrix products, arithmetic and copies ran while one was open for 39% -> 54% of each run, Pallas kernels for 0% -> 0%
where the time goes in v1:
time: 705 us; the launch traced here: 701 us
  matrix products  442 us (63%)
  waiting for transfers between devices  135 us (19%)
  local copies, waits for them, and re-layouts  72.3 us (10%)
  other arithmetic  29.7 us (4%)
  between operations  13.9 us (2%)
  starting transfers between devices  8.11 us (1%)
    dot_general x24, matrix products, per_device(): jnp.einsum('aijxz,awz->aijxw', inner[:, :, :, out_slot], right_side, prec...  186 us
    dot_general x8, matrix products, per_device(): jnp.einsum('axy,aijsyz->aijsxz', centre[:, term_index], amps, precision=l...  133 us
    dot_general x7, matrix products, per_device(): jnp.einsum('aiktu,akjuv->aijtv', piece[:, :, :, in_slot], cycle_rows, pre...  123 us
    ppermute x3, waiting for transfers between devices, field_plan(): piece_now = lax.ppermute(piece_now, axis_name=mesh_name, perm=x_new)  91.6 us
    unnamed x53, local copies, waits for them, and re-layouts  60.3 us
    all_gather x1, waiting for transfers between devices, per_device(): piece = lax.all_gather(amps, 'col', axis=2, tiled=True)  25.1 us
    mul x2, other arithmetic, per_device(): return keep_float * (integrals + ladder + cycle)  22.6 us
  transfers between devices with their start and end apart: 6, of which 4 were waited for; matrix products, arithmetic and copies ran while one was open for 54% of the time, Pallas kernels for 0%

profile of v1, /device:TPU:0, one launch (start us, length us, event | category | flops | bytes accessed | tf_op | source)
XLA Modules:
  0.0 700.8 jit_solution(4906817975415266654)
XLA Ops:
  27.3 14.0 %collective-permute-done = f32[1,11,128,128]{3,2,0,1:T(8,128)S(1)} collective-permute-done((f32[1,11,128,128]{3,2,0,1:T(8,128)S(1)}, f32[1,11,128,128]{3,2,0,1:T(8,128)S(1)}, u32[]{:S(2)}, u32[]{:S(2)}) %collective-permute-start) | collective-permute-done | bytes 720928 | tf_op jit(solution)/shard_map/ppermute | solution.py:34
  49.9 91.6 %collective-permute-done.2 = f32[42,1,1,3,128,128]{5,4,0,3,2,1:T(8,128)} collective-permute-done((f32[42,1,1,3,128,128]{5,4,0,3,2,1:T(8,128)S(1)}, f32[42,1,1,3,128,128]{5,4,0,3,2,1:T(8,128)}, u32[]{:S(2)}, u32[]{:S(2)}) %collective-permute-start.2) | collective-permute-done | bytes 8257568 | tf_op jit(solution)/shard_map/ppermute | solution.py:17
  141.7 18.1 %fusion.33 = f32[40,1,1,3,128,128]{4,5,3,0,2,1:T(8,128)S(1)} fusion(f32[40,3]{0,1:T(4,128)S(1)} %bitcast.502, f32[40,1,1,3,128,128]{5,4,3,2,1,0:T(8,128)} %param.5, f32[40,8,128,128]{3,2,1,0:T(8,128)} %param.8), kind=kOutput, calls=%fused_computation.49 | convolution fusion | flops 3021864960 | bytes 18350560 | tf_op jit(solution)/shard_map/axy,aijsyz->aijsxz/dot_general | solution.py:69
  162.9 8.0 %fusion.179 = f32[40,1,1,1,128,128]{5,4,0,3,2,1:T(8,128)} fusion(f32[40,1,1,3,128,128]{4,5,3,0,2,1:T(8,128)S(1)} %fusion.33, f32[40,8,128,128]{3,2,1,0:T(8,128)} %param.8), kind=kOutput, calls=%fused_computation.223 | convolution fusion | flops 1006632960 | bytes 7864320 | tf_op jit(solution)/shard_map/aijxz,awz->aijxw/dot_general | solution.py:76
  170.9 18.1 %fusion.36 = f32[40,1,1,3,128,128]{4,5,3,0,2,1:T(8,128)} fusion(f32[40,3]{0,1:T(4,128)S(1)} %bitcast.503, f32[40,1,1,3,128,128]{5,4,3,2,1,0:T(8,128)} %param.5, f32[40,8,128,128]{3,2,1,0:T(8,128)} %param.8), kind=kOutput, calls=%fused_computation.50 | convolution fusion | flops 3021864960 | bytes 18350560 | tf_op jit(solution)/shard_map/axy,aijsyz->aijsxz/dot_general | solution.py:69
  189.0 7.7 %fusion.184 = f32[40,1,1,1,128,128]{5,4,0,3,2,1:T(8,128)} fusion(f32[40,1,1,3,128,128]{4,5,3,0,2,1:T(8,128)} %fusion.36, f32[40,8,128,128]{3,2,1,0:T(8,128)S(1)} %bitcast.496), kind=kOutput, calls=%fused_computation.226 | convolution fusion | flops 1006632960 | bytes 7864320 | tf_op jit(solution)/shard_map/aijxz,awz->aijxw/dot_general | solution.py:76
  196.7 15.6 %fusion.39 = f32[40,1,1,3,128,128]{4,5,3,0,2,1:T(8,128)} fusion(f32[40,3]{0,1:T(4,128)S(1)} %bitcast.504, f32[40,1,1,3,128,128]{5,4,3,2,1,0:T(8,128)S(1)} %bitcast.498, f32[40,8,128,128]{3,2,1,0:T(8,128)S(1)} %bitcast.496), kind=kOutput, calls=%fused_computation.51 | convolution fusion | flops 3021864960 | bytes 18352128 | tf_op jit(solution)/shard_map/axy,aijsyz->aijsxz/dot_general | solution.py:69
  212.4 7.7 %fusion.189 = f32[40,1,1,1,128,128]{5,4,0,3,2,1:T(8,128)} fusion(f32[40,1,1,3,128,128]{4,5,3,0,2,1:T(8,128)} %fusion.39, f32[40,8,128,128]{3,2,1,0:T(8,128)S(1)} %bitcast.496), kind=kOutput, calls=%fused_computation.229 | convolution fusion | flops 1006632960 | bytes 7864320 | tf_op jit(solution)/shard_map/aijxz,awz->aijxw/dot_general | solution.py:76
  220.1 15.7 %fusion.42 = f32[40,1,1,3,128,128]{4,5,3,0,2,1:T(8,128)} fusion(f32[40,3]{0,1:T(4,128)S(1)} %bitcast.505, f32[40,1,1,3,128,128]{5,4,3,2,1,0:T(8,128)S(1)} %bitcast.498, f32[40,8,128,128]{3,2,1,0:T(8,128)S(1)} %bitcast.496), kind=kOutput, calls=%fused_computation.52 | convolution fusion | flops 3021864960 | bytes 18352128 | tf_op jit(solution)/shard_map/axy,aijsyz->aijsxz/dot_general | solution.py:69
  235.7 7.7 %fusion.194 = f32[40,1,1,1,128,128]{5,4,0,3,2,1:T(8,128)} fusion(f32[40,1,1,3,128,128]{4,5,3,0,2,1:T(8,128)} %fusion.42, f32[40,8,128,128]{3,2,1,0:T(8,128)S(1)} %bitcast.496), kind=kOutput, calls=%fused_computation.232 | convolution fusion | flops 1006632960 | bytes 7864320 | tf_op jit(solution)/shard_map/aijxz,awz->aijxw/dot_general | solution.py:76
  243.4 15.6 %fusion.45 = f32[40,1,1,3,128,128]{4,5,3,0,2,1:T(8,128)} fusion(f32[40,3]{0,1:T(4,128)S(1)} %bitcast.506, f32[40,1,1,3,128,128]{5,4,3,2,1,0:T(8,128)S(1)} %bitcast.498, f32[40,8,128,128]{3,2,1,0:T(8,128)S(1)} %bitcast.496), kind=kOutput, calls=%fused_computation.53 | convolution fusion | flops 3021864960 | bytes 18352128 | tf_op jit(solution)/shard_map/axy,aijsyz->aijsxz/dot_general | solution.py:69
  259.1 15.8 %fusion.48 = f32[40,1,1,3,128,128]{4,5,3,0,2,1:T(8,128)} fusion(f32[40,3]{0,1:T(4,128)S(1)} %bitcast.507, f32[40,1,1,3,128,128]{5,4,3,2,1,0:T(8,128)S(1)} %bitcast.498, f32[40,8,128,128]{3,2,1,0:T(8,128)S(1)} %bitcast.496), kind=kOutput, calls=%fused_computation.54 | convolution fusion | flops 3021864960 | bytes 18352128 | tf_op jit(solution)/shard_map/axy,aijsyz->aijsxz/dot_general | solution.py:69
  276.6 7.6 %fusion.199 = f32[40,1,1,1,128,128]{5,4,0,3,2,1:T(8,128)} fusion(f32[40,1,1,3,128,128]{4,5,3,0,2,1:T(8,128)} %fusion.45, f32[40,8,128,128]{3,2,1,0:T(8,128)S(1)} %bitcast.496), kind=kOutput, calls=%fused_computation.235 | convolution fusion | flops 1006632960 | bytes 7864320 | tf_op jit(solution)/shard_map/aijxz,awz->aijxw/dot_general | solution.py:76
  284.2 7.6 %fusion.204 = f32[40,1,1,1,128,128]{5,4,0,3,2,1:T(8,128)} fusion(f32[40,1,1,3,128,128]{4,5,3,0,2,1:T(8,128)} %fusion.48, f32[40,8,128,128]{3,2,1,0:T(8,128)S(1)} %bitcast.496), kind=kOutput, calls=%fused_computation.238 | convolution fusion | flops 1006632960 | bytes 7864320 | tf_op jit(solution)/shard_map/aijxz,awz->aijxw/dot_general | solution.py:76
  291.9 15.7 %fusion.51 = f32[40,1,1,3,128,128]{4,5,3,0,2,1:T(8,128)} fusion(f32[40,3]{0,1:T(4,128)S(1)} %bitcast.508, f32[40,1,1,3,128,128]{5,4,3,2,1,0:T(8,128)S(1)} %bitcast.498, f32[40,8,128,128]{3,2,1,0:T(8,128)S(1)} %bitcast.496), kind=kOutput, calls=%fused_computation.55 | convolution fusion | flops 3021864960 | bytes 18352128 | tf_op jit(solution)/shard_map/axy,aijsyz->aijsxz/dot_general | solution.py:69
  307.6 7.8 %fusion.209 = f32[40,1,1,1,128,128]{5,4,0,3,2,1:T(8,128)} fusion(f32[40,1,1,3,128,128]{4,5,3,0,2,1:T(8,128)} %fusion.51, f32[40,8,128,128]{3,2,1,0:T(8,128)S(1)} %bitcast.496), kind=kOutput, calls=%fused_computation.241 | convolution fusion | flops 1006632960 | bytes 7864320 | tf_op jit(solution)/shard_map/aijxz,awz->aijxw/dot_general | solution.py:76
  315.4 18.3 %fusion.54 = f32[40,1,1,3,128,128]{4,5,3,0,2,1:T(8,128)} fusion(f32[40,3]{0,1:T(4,128)S(1)} %bitcast.509, f32[40,1,1,3,128,128]{5,4,3,2,1,0:T(8,128)} %param.5, f32[40,8,128,128]{3,2,1,0:T(8,128)S(1)} %bitcast.496), kind=kOutput, calls=%fused_computation.56 | convolution fusion | flops 3021864960 | bytes 18352128 | tf_op jit(solution)/shard_map/axy,aijsyz->aijsxz/dot_general | solution.py:69
  333.7 7.7 %fusion.216 = f32[40,1,1,1,128,128]{5,4,0,3,2,1:T(8,128)} fusion(f32[40,1,1,3,128,128]{4,5,3,0,2,1:T(8,128)} %fusion.54, f32[40,8,128,128]{3,2,1,0:T(8,128)S(1)} %bitcast.496), kind=kOutput, calls=%fused_computation.244 | convolution fusion | flops 1006632960 | bytes 7864320 | tf_op jit(solution)/shard_map/aijxz,awz->aijxw/dot_general | solution.py:76
  341.4 7.7 %fusion.183 = f32[40,1,1,1,128,128]{5,4,0,3,2,1:T(8,128)} fusion(f32[1,11,128,128]{3,2,0,1:T(8,128)S(1)} %collective-permute-done, f32[40,3,128,128]{3,2,0,1:T(8,128)S(1)} %bitcast.479, f32[40,1,1,3,128,128]{4,5,3,0,2,1:T(8,128)} %fusion.36, f32[40,8,128,128]{3,2,1,0:T(8,128)S(1)} %bitcast.496), kind=kOutput, calls=%fused_computation.225 | convolution fusion | flops 1007943680 | bytes 34799616 | tf_op jit(solution)/shard_map/aijxz,awz->aijxw/dot_general | solution.py:76
  349.1 7.9 %fusion.187 = f32[40,1,1,1,128,128]{5,4,0,3,2,1:T(8,128)} fusion(f32[1,11,128,128]{3,2,0,1:T(8,128)S(1)} %collective-permute-done.1, f32[40,3,128,128]{3,2,0,1:T(8,128)S(1)} %bitcast.480, f32[40,1,1,3,128,128]{4,5,3,0,2,1:T(8,128)} %fusion.36, f32[40,8,128,128]{3,2,1,0:T(8,128)S(1)} %bitcast.496), kind=kOutput, calls=%fused_computation.227 | convolution fusion | flops 1007943680 | bytes 34799616 | tf_op jit(solution)/shard_map/aijxz,awz->aijxw/dot_general | solution.py:76
  357.0 7.6 %fusion.188 = f32[40,1,1,1,128,128]{5,4,0,3,2,1:T(8,128)} fusion(f32[1,11,128,128]{3,2,0,1:T(8,128)S(1)} %collective-permute-done, f32[40,3,128,128]{3,2,0,1:T(8,128)S(1)} %bitcast.481, f32[40,1,1,3,128,128]{4,5,3,0,2,1:T(8,128)} %fusion.39, f32[40,8,128,128]{3,2,1,0:T(8,128)S(1)} %bitcast.496), kind=kOutput, calls=%fused_computation.228 | convolution fusion | flops 1007943680 | bytes 34799616 | tf_op jit(solution)/shard_map/aijxz,awz->aijxw/dot_general | solution.py:76
  364.6 7.7 %fusion.192 = f32[40,1,1,1,128,128]{5,4,0,3,2,1:T(8,128)} fusion(f32[1,11,128,128]{3,2,0,1:T(8,128)S(1)} %collective-permute-done.1, f32[40,3,128,128]{3,2,0,1:T(8,128)S(1)} %bitcast.482, f32[40,1,1,3,128,128]{4,5,3,0,2,1:T(8,128)} %fusion.39, f32[40,8,128,128]{3,2,1,0:T(8,128)S(1)} %bitcast.496), kind=kOutput, calls=%fused_computation.230 | convolution fusion | flops 1007943680 | bytes 34799616 | tf_op jit(solution)/shard_map/aijxz,awz->aijxw/dot_general | solution.py:76
  372.3 8.1 %fusion.193 = f32[40,1,1,1,128,128]{5,4,0,3,2,1:T(8,128)} fusion(f32[1,11,128,128]{3,2,0,1:T(8,128)S(1)} %collective-permute-done, f32[40,3,128,128]{3,2,0,1:T(8,128)S(1)} %bitcast.483, f32[40,1,1,3,128,128]{4,5,3,0,2,1:T(8,128)} %fusion.42, f32[40,8,128,128]{3,2,1,0:T(8,128)S(1)} %bitcast.496), kind=kOutput, calls=%fused_computation.231 | convolution fusion | flops 1007943680 | bytes 34799616 | tf_op jit(solution)/shard_map/aijxz,awz->aijxw/dot_general | solution.py:76
  380.4 7.7 %fusion.197 = f32[40,1,1,1,128,128]{5,4,0,3,2,1:T(8,128)} fusion(f32[1,11,128,128]{3,2,0,1:T(8,128)S(1)} %collective-permute-done.1, f32[40,3,128,128]{3,2,0,1:T(8,128)S(1)} %bitcast.484, f32[40,1,1,3,128,128]{4,5,3,0,2,1:T(8,128)} %fusion.42, f32[40,8,128,128]{3,2,1,0:T(8,128)S(1)} %bitcast.496), kind=kOutput, calls=%fused_computation.233 | convolution fusion | flops 1007943680 | bytes 34799616 | tf_op jit(solution)/shard_map/aijxz,awz->aijxw/dot_general | solution.py:76
  388.1 7.6 %fusion.198 = f32[40,1,1,1,128,128]{5,4,0,3,2,1:T(8,128)} fusion(f32[1,11,128,128]{3,2,0,1:T(8,128)S(1)} %collective-permute-done, f32[40,3,128,128]{3,2,0,1:T(8,128)S(1)} %bitcast.485, f32[40,1,1,3,128,128]{4,5,3,0,2,1:T(8,128)} %fusion.45, f32[40,8,128,128]{3,2,1,0:T(8,128)S(1)} %bitcast.496), kind=kOutput, calls=%fused_computation.234 | convolution fusion | flops 1007943680 | bytes 34799616 | tf_op jit(solution)/shard_map/aijxz,awz->aijxw/dot_general | solution.py:76
  395.7 7.9 %fusion.202 = f32[40,1,1,1,128,128]{5,4,0,3,2,1:T(8,128)} fusion(f32[1,11,128,128]{3,2,0,1:T(8,128)S(1)} %collective-permute-done.1, f32[40,3,128,128]{3,2,0,1:T(8,128)S(1)} %bitcast.486, f32[40,1,1,3,128,128]{4,5,3,0,2,1:T(8,128)} %fusion.45, f32[40,8,128,128]{3,2,1,0:T(8,128)S(1)} %bitcast.496), kind=kOutput, calls=%fused_computation.236 | convolution fusion | flops 1007943680 | bytes 34799616 | tf_op jit(solution)/shard_map/aijxz,awz->aijxw/dot_general | solution.py:76
  403.7 7.7 %fusion.203 = f32[40,1,1,1,128,128]{5,4,0,3,2,1:T(8,128)} fusion(f32[1,11,128,128]{3,2,0,1:T(8,128)S(1)} %collective-permute-done, f32[40,3,128,128]{3,2,0,1:T(8,128)S(1)} %bitcast.487, f32[40,1,1,3,128,128]{4,5,3,0,2,1:T(8,128)} %fusion.48, f32[40,8,128,128]{3,2,1,0:T(8,128)S(1)} %bitcast.496), kind=kOutput, calls=%fused_computation.237 | convolution fusion | flops 1007943680 | bytes 34799616 | tf_op jit(solution)/shard_map/aijxz,awz->aijxw/dot_general | solution.py:76
  411.3 7.9 %fusion.207 = f32[40,1,1,1,128,128]{5,4,0,3,2,1:T(8,128)} fusion(f32[1,11,128,128]{3,2,0,1:T(8,128)S(1)} %collective-permute-done.1, f32[40,3,128,128]{3,2,0,1:T(8,128)S(1)} %bitcast.488, f32[40,1,1,3,128,128]{4,5,3,0,2,1:T(8,128)} %fusion.48, f32[40,8,128,128]{3,2,1,0:T(8,128)S(1)} %bitcast.496), kind=kOutput, calls=%fused_computation.239 | convolution fusion | flops 1007943680 | bytes 34799616 | tf_op jit(solution)/shard_map/aijxz,awz->aijxw/dot_general | solution.py:76
  419.2 7.7 %fusion.208 = f32[40,1,1,1,128,128]{5,4,0,3,2,1:T(8,128)} fusion(f32[1,11,128,128]{3,2,0,1:T(8,128)S(1)} %collective-permute-done, f32[40,3,128,128]{3,2,0,1:T(8,128)S(1)} %bitcast.489, f32[40,1,1,3,128,128]{4,5,3,0,2,1:T(8,128)} %fusion.51, f32[40,8,128,128]{3,2,1,0:T(8,128)S(1)} %bitcast.496), kind=kOutput, calls=%fused_computation.240 | convolution fusion | flops 1007943680 | bytes 34799616 | tf_op jit(solution)/shard_map/aijxz,awz->aijxw/dot_general | solution.py:76
  426.9 7.6 %fusion.212 = f32[40,1,1,1,128,128]{5,4,0,3,2,1:T(8,128)} fusion(f32[1,11,128,128]{3,2,0,1:T(8,128)S(1)} %collective-permute-done.1, f32[40,3,128,128]{3,2,0,1:T(8,128)S(1)} %bitcast.490, f32[40,1,1,3,128,128]{4,5,3,0,2,1:T(8,128)} %fusion.51, f32[40,8,128,128]{3,2,1,0:T(8,128)S(1)} %bitcast.496), kind=kOutput, calls=%fused_computation.242 | convolution fusion | flops 1007943680 | bytes 34799616 | tf_op jit(solution)/shard_map/aijxz,awz->aijxw/dot_general | solution.py:76
  434.5 8.0 %fusion.213 = f32[40,1,1,1,128,128]{5,4,0,3,2,1:T(8,128)} fusion(f32[1,11,128,128]{3,2,0,1:T(8,128)S(1)} %collective-permute-done, f32[40,3,128,128]{3,2,0,1:T(8,128)S(1)} %bitcast.491, f32[40,1,1,3,128,128]{4,5,3,0,2,1:T(8,128)} %fusion.54, f32[40,8,128,128]{3,2,1,0:T(8,128)S(1)} %bitcast.496), kind=kOutput, calls=%fused_computation.243 | convolution fusion | flops 1007943680 | bytes 34799616 | tf_op jit(solution)/shard_map/aijxz,awz->aijxw/dot_general | solution.py:76
  442.6 7.7 %fusion.219 = f32[40,1,1,1,128,128]{5,4,0,3,2,1:T(8,128)} fusion(f32[1,11,128,128]{3,2,0,1:T(8,128)S(1)} %collective-permute-done.1, f32[40,3,128,128]{3,2,0,1:T(8,128)S(1)} %bitcast.492, f32[40,1,1,3,128,128]{4,5,3,0,2,1:T(8,128)} %fusion.54, f32[40,8,128,128]{3,2,1,0:T(8,128)S(1)} %bitcast.496), kind=kOutput, calls=%fused_computation.245 | convolution fusion | flops 1007943680 | bytes 34799616 | tf_op jit(solution)/shard_map/aijxz,awz->aijxw/dot_general | solution.py:76
  450.3 7.6 %fusion.178 = f32[40,1,1,1,128,128]{5,4,0,3,2,1:T(8,128)} fusion(f32[1,11,128,128]{3,2,0,1:T(8,128)S(1)} %collective-permute-done, f32[40,3,128,128]{3,2,0,1:T(8,128)S(1)} %bitcast.493, f32[40,1,1,3,128,128]{4,5,3,0,2,1:T(8,128)} %copy-done.2, f32[40,8,128,128]{3,2,1,0:T(8,128)S(1)} %bitcast.496), kind=kOutput, calls=%fused_computation.222 | convolution fusion | flops 1007943680 | bytes 34799616 | tf_op jit(solution)/shard_map/aijxz,awz->aijxw/dot_general | solution.py:76
  457.9 7.8 %fusion.182 = f32[40,1,1,1,128,128]{5,4,0,3,2,1:T(8,128)} fusion(f32[1,11,128,128]{3,2,0,1:T(8,128)S(1)} %collective-permute-done.1, f32[40,3,128,128]{3,2,0,1:T(8,128)S(1)} %bitcast.494, f32[40,1,1,3,128,128]{4,5,3,0,2,1:T(8,128)} %copy-done.2, f32[40,8,128,128]{3,2,1,0:T(8,128)S(1)} %bitcast.496), kind=kOutput, calls=%fused_computation.224 | convolution fusion | flops 1007943680 | bytes 34799616 | tf_op jit(solution)/shard_map/aijxz,awz->aijxw/dot_general | solution.py:76
  465.7 7.7 %constant_dynamic-update-slice_fusion.7 = f32[42,8,1,3,128,128]{5,4,0,3,2,1:T(8,128)} fusion(f32[42,1,1,3,128,128]{5,4,0,3,2,1:T(8,128)} %collective-permute-done.4), kind=kLoop, calls=%fused_computation.255 | loop fusion | bytes 16515072
  473.4 7.8 %constant_dynamic-update-slice_fusion.6 = f32[42,8,1,3,128,128]{5,4,0,3,2,1:T(8,128)} fusion(f32[42,8,1,3,128,128]{5,4,0,3,2,1:T(8,128)} %constant_dynamic-update-slice_fusion.7, f32[42,1,1,3,128,128]{5,4,0,3,2,1:T(8,128)} %collective-permute-done.3), kind=kLoop, calls=%fused_computation.254 | loop fusion | bytes 16515072
  481.1 7.8 %constant_dynamic-update-slice_fusion.5 = f32[42,8,1,3,128,128]{5,4,0,3,2,1:T(8,128)} fusion(f32[42,8,1,3,128,128]{5,4,0,3,2,1:T(8,128)} %constant_dynamic-update-slice_fusion.6, f32[42,1,1,3,128,128]{5,4,0,3,2,1:T(8,128)} %collective-permute-done.2), kind=kLoop, calls=%fused_computation.253 | loop fusion | bytes 16515072
  493.1 7.6 %constant_dynamic-update-slice_fusion.3 = f32[42,8,1,3,128,128]{5,4,0,3,2,1:T(8,128)} fusion(f32[42,8,1,3,128,128]{5,4,0,3,2,1:T(8,128)} %constant_dynamic-update-slice_fusion.4, f32[42,1,1,3,128,128]{5,4,0,3,2,1:T(8,128)} %collective-permute-done.4), kind=kLoop, calls=%fused_computation.251 | loop fusion | bytes 16515072
  500.7 7.6 %constant_dynamic-update-slice_fusion.2 = f32[42,8,1,3,128,128]{5,4,0,3,2,1:T(8,128)} fusion(f32[42,8,1,3,128,128]{5,4,0,3,2,1:T(8,128)} %constant_dynamic-update-slice_fusion.3, f32[42,1,1,3,128,128]{5,4,0,3,2,1:T(8,128)} %collective-permute-done.3), kind=kLoop, calls=%fused_computation.250 | loop fusion | bytes 16515072
  520.1 25.1 %all-gather.2.cloned.1.call-done = f32[40,1,4,3,128,128]{5,4,3,1,0,2:T(8,128)} async-done(((f32[40,1,1,3,128,128]{5,4,3,1,0,2:T(8,128)}), f32[40,1,4,3,128,128]{5,4,3,1,0,2:T(8,128)}) %all-gather.2.cloned.1.call-update) | async-done | bytes 31457296 | tf_op jit(solution)/shard_map/all_gather | solution.py:84
  545.2 16.2 %fusion.6 = f32[40,128,128,1]{1,2,0,3:T(8,128)S(1)} fusion(f32[42,8,1,3,128,128]{5,4,0,3,2,1:T(8,128)} %constant_dynamic-update-slice_fusion, s32[]{:T(128)S(6)} %select_n.14, s32[]{:T(128)S(6)} %add.193, f32[40,1,4,3,128,128]{5,4,3,1,0,2:T(8,128)} %all-gather.2.cloned.1.call-done), kind=kOutput, calls=%fused_computation.16 | convolution fusion | flops 4026531840 | bytes 23592968 | tf_op jit(solution)/shard_map/aiktu,akjuv->aijtv/dot_general | solution.py:92
  561.4 17.6 %fusion.3 = f32[40,128,128,1]{1,2,0,3:T(8,128)} fusion(f32[42,8,1,3,128,128]{5,4,0,3,2,1:T(8,128)} %constant_dynamic-update-slice_fusion, s32[]{:T(128)S(6)} %add.193, s32[]{:T(128)S(6)} %select_n.14, f32[40,1,4,3,128,128]{5,4,3,1,0,2:T(8,128)} %all-gather.2.cloned.1.call-done), kind=kOutput, calls=%fused_computation.8 | convolution fusion | flops 4026531840 | bytes 23592968 | tf_op jit(solution)/shard_map/aiktu,akjuv->aijtv/dot_general | solution.py:92
  578.9 17.6 %fusion.4 = f32[40,128,128,1]{1,2,0,3:T(8,128)} fusion(f32[42,8,1,3,128,128]{5,4,0,3,2,1:T(8,128)} %constant_dynamic-update-slice_fusion, s32[]{:T(128)S(6)} %select_n.14, s32[]{:T(128)S(6)} %add.195, f32[40,1,4,3,128,128]{5,4,3,1,0,2:T(8,128)} %all-gather.2.cloned.1.call-done), kind=kOutput, calls=%fused_computation.10 | convolution fusion | flops 4026531840 | bytes 23592968 | tf_op jit(solution)/shard_map/aiktu,akjuv->aijtv/dot_general | solution.py:92
  596.5 16.4 %fusion.1 = f32[40,128,128,1]{1,2,0,3:T(8,128)S(1)} fusion(f32[42,8,1,3,128,128]{5,4,0,3,2,1:T(8,128)} %constant_dynamic-update-slice_fusion, s32[]{:T(128)S(6)} %add.193, s32[]{:T(128)S(6)} %select_n.14, s32[]{:T(128)S(6)} %add.195, f32[40,1,4,3,128,128]{5,4,3,1,0,2:T(8,128)} %all-gather.2.cloned.1.call-done), kind=kOutput, calls=%fused_computation.3 | convolution fusion | flops 4026531840 | bytes 23592972 | tf_op jit(solution)/shard_map/aiktu,akjuv->aijtv/dot_general | solution.py:92
  613.0 17.8 %fusion.153 = f32[40,1,1,1,128,128]{5,4,0,3,2,1:T(8,128)} fusion(f32[40,128,128,1]{1,2,0,3:T(8,128)S(1)} %fusion.6, f32[40,1,4,3,128,128]{5,4,3,1,0,2:T(8,128)} %all-gather.2.cloned.1.call-done, f32[42,8,1,3,128,128]{5,4,0,3,2,1:T(8,128)} %constant_dynamic-update-slice_fusion, s32[]{:T(128)S(6)} %add.193, s32[]{:T(128)S(6)} %select_n.14), kind=kOutput, calls=%fused_computation.197 | convolution fusion | flops 4027187200 | bytes 26214408 | tf_op jit(solution)/shard_map/aiktu,akjuv->aijtv/dot_general | solution.py:92
  630.8 18.0 %fusion.151 = f32[40,1,1,1,128,128]{5,4,0,3,2,1:T(8,128)} fusion(f32[40,128,128,1]{1,2,0,3:T(8,128)S(1)} %fusion.1, f32[40,1,4,3,128,128]{5,4,3,1,0,2:T(8,128)} %all-gather.2.cloned.1.call-done, f32[42,8,1,3,128,128]{5,4,0,3,2,1:T(8,128)} %constant_dynamic-update-slice_fusion, s32[]{:T(128)S(6)} %add.195, s32[]{:T(128)S(6)} %select_n.14, s32[]{:T(128)S(6)} %add.193), kind=kOutput, calls=%fused_computation.192 | convolution fusion | flops 4027187200 | bytes 26214412 | tf_op jit(solution)/shard_map/aiktu,akjuv->aijtv/dot_general | solution.py:92
  648.8 19.2 %fusion.152 = f32[40,1,1,1,128,128]{5,4,0,3,2,1:T(8,128)} fusion(f32[40,128,128,1]{1,2,0,3:T(8,128)S(1)} %copy-done.8, f32[40,128,128,1]{1,2,0,3:T(8,128)} %fusion.4, f32[40,1,4,3,128,128]{5,4,3,1,0,2:T(8,128)} %all-gather.2.cloned.1.call-done, f32[42,8,1,3,128,128]{5,4,0,3,2,1:T(8,128)} %constant_dynamic-update-slice_fusion, s32[]{:T(128)S(6)} %add.195, ...), kind=kOutput, calls=%fused_computation.194 | convolution fusion | flops 4027842560 | bytes 28835848 | tf_op jit(solution)/shard_map/aiktu,akjuv->aijtv/dot_general | solution.py:92
  668.0 21.9 %fusion.16 = f32[40,1,1,3,128,128]{5,4,0,3,2,1:T(8,128)S(1)} fusion(f32[40,1,1,1,128,128]{5,4,0,3,2,1:T(8,128)} %fusion.182, f32[40,1,1,1,128,128]{5,4,0,3,2,1:T(8,128)} %fusion.179, f32[40,1,1,1,128,128]{5,4,0,3,2,1:T(8,128)} %fusion.178, f32[40,1,1,1,128,128]{5,4,0,3,2,1:T(8,128)S(1)} %copy-done.4, f32[40,1,1,1,128,128]{5,4,0,3,2,1:T(8,128)} %fusion.184, ...), kind=kLoop, calls=%fused_computation.30 | loop fusion | flops 55050240 | bytes 86508000 | tf_op jit(solution)/shard_map/mul | solution.py:100
  (71 shorter events, 54.0 us)
Async XLA Ops:
  6.5 538.6 %all-gather.2.cloned.1.call-start = ((), (), s32[]{:S(2)}) async-start(), calls=%async_computation | async-start | bytes 39321600 | tf_op jit(solution)/shard_map/all_gather | solution.py:84
  7.3 308.1 %copy-start.9 = (f32[40,1,1,3]{0,3,2,1:T(4,128)}, f32[40,1,1,3]{0,3,2,1:T(4,128)S(1)}, u32[]{:S(2)}) copy-start(f32[40,1,1,3]{0,3,2,1:T(4,128)S(1)} %copy.369) | copy-start | bytes 1444
  19.0 26.5 %copy-start = (f32[40,1,1,3,128,128]{5,4,0,3,2,1:T(8,128)}, f32[40,1,1,3,128,128]{5,4,0,3,2,1:T(8,128)S(1)}, u32[]{:S(2)}) copy-start(f32[40,1,1,3,128,128]{5,4,0,3,2,1:T(8,128)S(1)} %copy.368) | copy-start | bytes 23592964
  21.1 20.3 %collective-permute-start = (f32[1,11,128,128]{3,2,0,1:T(8,128)S(1)}, f32[1,11,128,128]{3,2,0,1:T(8,128)S(1)}, u32[]{:S(2)}, u32[]{:S(2)}) collective-permute-start(f32[1,11,128,128]{3,2,0,1:T(8,128)S(1)} %get-tuple-element.5), channel_id=1, source_target_pairs={{0,1},{2,3},{4,5},{6,7},{8,9},{10,11},{12,13},{14,15},{16,17},{18,... | collective-permute-start | bytes 2162696 | tf_op jit(solution)/shard_map/ppermute | solution.py:34
  26.0 19.5 %collective-permute-start.1 = (f32[1,11,128,128]{3,2,0,1:T(8,128)S(1)}, f32[1,11,128,128]{3,2,0,1:T(8,128)S(1)}, u32[]{:S(2)}, u32[]{:S(2)}) collective-permute-start(f32[1,11,128,128]{3,2,0,1:T(8,128)S(1)} %get-tuple-element.6), channel_id=1, source_target_pairs={{1,0},{3,2},{5,4},{7,6},{9,8},{11,10},{13,12},{15,14},{17,16},{19,... | collective-permute-start | bytes 2162696 | tf_op jit(solution)/shard_map/ppermute | solution.py:37
  46.7 3.2 copy-start.1
  49.9 91.6 %collective-permute-start.2 = (f32[42,1,1,3,128,128]{5,4,0,3,2,1:T(8,128)S(1)}, f32[42,1,1,3,128,128]{5,4,0,3,2,1:T(8,128)}, u32[]{:S(2)}, u32[]{:S(2)}) collective-permute-start(f32[42,1,1,3,128,128]{5,4,0,3,2,1:T(8,128)S(1)} %fusion.7), channel_id=1, source_target_pairs={{0,8},{8,16},{16,24},{24,0},{1,9},{9,17},{17,25},{25,1},{2,10},{10... | collective-permute-start | bytes 24772616 | tf_op jit(solution)/shard_map/ppermute | solution.py:17
  141.5 133.4 %collective-permute-start.3 = (f32[42,1,1,3,128,128]{5,4,0,3,2,1:T(8,128)}, f32[42,1,1,3,128,128]{5,4,0,3,2,1:T(8,128)}, u32[]{:S(2)}, u32[]{:S(2)}) collective-permute-start(f32[42,1,1,3,128,128]{5,4,0,3,2,1:T(8,128)} %collective-permute-done.2), channel_id=1, source_target_pairs={{0,8},{8,16},{16,24},{24,0},{1,9},{9,17},{17,25},{25,1},{2,10},{10... | collective-permute-start | bytes 24772616 | tf_op jit(solution)/shard_map/ppermute | solution.py:17
  141.7 47.3 %slice-start.2 = ((s8[20971520]{0:T(1024)(128)(4,1)}), s8[4194304]{0:T(1024)(128)(4,1)S(1)}, s32[]{:S(2)}) async-start(s8[20971520]{0:T(1024)(128)(4,1)} %bitcast.495), calls=%async_computation.3 | async-start | bytes 8388608
  141.7 47.3 %slice-start.3 = ((s8[20971520]{0:T(1024)(128)(4,1)}), s8[4194304]{0:T(1024)(128)(4,1)S(1)}, s32[]{:S(2)}) async-start(s8[20971520]{0:T(1024)(128)(4,1)} %bitcast.495), calls=%async_computation.4 | async-start | bytes 8388608
  141.7 47.3 %slice-start.4 = ((s8[20971520]{0:T(1024)(128)(4,1)}), s8[4194304]{0:T(1024)(128)(4,1)S(1)}, s32[]{:S(2)}) async-start(s8[20971520]{0:T(1024)(128)(4,1)} %bitcast.495), calls=%async_computation.5 | async-start | bytes 8388608
  159.8 3.1 copy-start.2
  162.9 33.8 %slice-start.7 = ((s8[7864320]{0:T(1024)(128)(4,1)}), s8[4194304]{0:T(1024)(128)(4,1)S(1)}, s32[]{:S(2)}) async-start(s8[7864320]{0:T(1024)(128)(4,1)} %bitcast.497), calls=%async_computation.8 | async-start | bytes 8388608
  170.9 18.1 %slice-start.5 = ((s8[20971520]{0:T(1024)(128)(4,1)}), s8[4194304]{0:T(1024)(128)(4,1)S(1)}, s32[]{:S(2)}) async-start(s8[20971520]{0:T(1024)(128)(4,1)} %bitcast.495), calls=%async_computation.6 | async-start | bytes 8388608
  170.9 18.1 %slice-start.6 = ((s8[20971520]{0:T(1024)(128)(4,1)}), s8[4194304]{0:T(1024)(128)(4,1)S(1)}, s32[]{:S(2)}) async-start(s8[20971520]{0:T(1024)(128)(4,1)} %bitcast.495), calls=%async_computation.7 | async-start | bytes 8388608
  170.9 25.9 %slice-start.8 = ((s8[7864320]{0:T(1024)(128)(4,1)}), s8[3670016]{0:T(1024)(128)(4,1)S(1)}, s32[]{:S(2)}) async-start(s8[7864320]{0:T(1024)(128)(4,1)} %bitcast.497), calls=%async_computation.9 | async-start | bytes 7340032
  274.9 190.8 %collective-permute-start.4 = (f32[42,1,1,3,128,128]{5,4,0,3,2,1:T(8,128)}, f32[42,1,1,3,128,128]{5,4,0,3,2,1:T(8,128)}, u32[]{:S(2)}, u32[]{:S(2)}) collective-permute-start(f32[42,1,1,3,128,128]{5,4,0,3,2,1:T(8,128)} %collective-permute-done.3), channel_id=1, source_target_pairs={{0,8},{8,16},{16,24},{24,0},{1,9},{9,17},{17,25},{25,1},{2,10},{10... | collective-permute-start | bytes 24772616 | tf_op jit(solution)/shard_map/ppermute | solution.py:17
  307.6 33.9 %slice-start = ((s8[7864320]{0:T(1024)(128)(4,1)}), s8[4194304]{0:T(1024)(128)(4,1)S(1)}, s32[]{:S(2)}) async-start(s8[7864320]{0:T(1024)(128)(4,1)} %bitcast.477), calls=%async_computation.1 | async-start | bytes 8388608
  315.4 26.1 %slice-start.1 = ((s8[7864320]{0:T(1024)(128)(4,1)}), s8[3670016]{0:T(1024)(128)(4,1)S(1)}, s32[]{:S(2)}) async-start(s8[7864320]{0:T(1024)(128)(4,1)} %bitcast.477), calls=%async_computation.2 | async-start | bytes 7340032
  473.4 15.5 %slice-start.9 = ((s8[8257536]{0:T(1024)(128)(4,1)}), s8[4194304]{0:T(1024)(128)(4,1)S(1)}, s32[]{:S(2)}) async-start(s8[8257536]{0:T(1024)(128)(4,1)} %bitcast.499), calls=%async_computation.10 | async-start | bytes 8388608
  481.1 7.8 %slice-start.10 = ((s8[8257536]{0:T(1024)(128)(4,1)}), s8[4063232]{0:T(1024)(128)(4,1)S(1)}, s32[]{:S(2)}) async-start(s8[8257536]{0:T(1024)(128)(4,1)} %bitcast.499), calls=%async_computation.11 | async-start | bytes 8126464
  630.8 18.0 %copy-start.8 = (f32[40,128,128,1]{1,2,0,3:T(8,128)S(1)}, f32[40,128,128,1]{1,2,0,3:T(8,128)}, u32[]{:S(2)}) copy-start(f32[40,128,128,1]{1,2,0,3:T(8,128)} %fusion.3) | copy-start | bytes 7864324
  648.7 19.3 %copy-start.3 = (f32[40,1,1,1,128,128]{5,4,0,3,2,1:T(8,128)S(1)}, f32[40,1,1,1,128,128]{5,4,0,3,2,1:T(8,128)}, u32[]{:S(2)}) copy-start(f32[40,1,1,1,128,128]{5,4,0,3,2,1:T(8,128)} %fusion.183) | copy-start | bytes 7864324
  648.7 19.3 %copy-start.4 = (f32[40,1,1,1,128,128]{5,4,0,3,2,1:T(8,128)S(1)}, f32[40,1,1,1,128,128]{5,4,0,3,2,1:T(8,128)}, u32[]{:S(2)}) copy-start(f32[40,1,1,1,128,128]{5,4,0,3,2,1:T(8,128)} %fusion.187) | copy-start | bytes 7864324
  648.7 19.3 %copy-start.5 = (f32[40,1,1,1,128,128]{5,4,0,3,2,1:T(8,128)S(1)}, f32[40,1,1,1,128,128]{5,4,0,3,2,1:T(8,128)}, u32[]{:S(2)}) copy-start(f32[40,1,1,1,128,128]{5,4,0,3,2,1:T(8,128)} %fusion.188) | copy-start | bytes 7864324
  648.7 19.3 %copy-start.6 = (f32[40,1,1,1,128,128]{5,4,0,3,2,1:T(8,128)S(1)}, f32[40,1,1,1,128,128]{5,4,0,3,2,1:T(8,128)}, u32[]{:S(2)}) copy-start(f32[40,1,1,1,128,128]{5,4,0,3,2,1:T(8,128)} %fusion.192) | copy-start | bytes 7864324
  648.7 19.3 %copy-start.7 = (f32[40,1,1,1,128,128]{5,4,0,3,2,1:T(8,128)S(1)}, f32[40,1,1,1,128,128]{5,4,0,3,2,1:T(8,128)}, u32[]{:S(2)}) copy-start(f32[40,1,1,1,128,128]{5,4,0,3,2,1:T(8,128)} %fusion.193) | copy-start | bytes 7864324
  648.8 19.3 %copy-start.10 = (f32[40,1,1,3]{0,3,2,1:T(4,128)S(1)}, f32[40,1,1,3]{0,3,2,1:T(4,128)}, u32[]{:S(2)}) copy-start(f32[40,1,1,3]{0,3,2,1:T(4,128)} %copy-done.9) | copy-start | bytes 1444
Sparse Core Ops, SparseCore 0:
  15.3 529.8 all-gather.1
